TPU v7x, 32 devices: a whole 2x2x4 slice. The times are simulated.
32 devices in a mesh: parts: 2 (over x), seq: 16 (over z, y, core).
Axes of the slice: x: 2, y: 2, z: 4, core: 2. Of those that a mesh axis runs over, the one named last changes fastest.
Arguments:
- queries: bfloat16 [3072, 1024], P(('parts', 'seq')), parts along dimension 0, may hold values from -8 to 8
- self_keys: bfloat16 [3072, 1024], P(('parts', 'seq')), parts along dimension 0, may hold values from -8 to 8
- self_values: bfloat16 [3072, 1024], P(('parts', 'seq')), parts along dimension 0, may hold values from -8 to 8
- residual_in: bfloat16 [3072, 1024], P(('parts', 'seq')), parts along dimension 0, may hold values from -0.23925781 to 0.23925781
- text_keys: bfloat16 [2, 8, 256, 1024], P(None, 'parts', None, 'seq'), parts along dimension 1, may hold values from -8 to 8
- text_values: bfloat16 [2, 8, 256, 1024], P(None, 'parts', None, 'seq'), parts along dimension 1, may hold values from -8 to 8
- text_lengths: int32 [2, 8], P(None, 'parts'), parts along dimension 1, may hold values from 2 to 256
- frame_counts: int32 [8], P('parts'), parts along dimension 0, may hold values from 1 to 16, 24 in all
- mod_gain: float32 [1024], replicated, may hold values from 0.1 to 1.9
- mod_shift: float32 [1024], replicated, may hold values from -1.8 to 1.8
- head_weight: bfloat16 [1024, 64], replicated, may hold values from -0.1875 to 0.1875
- head_bias: float32 [64], replicated, may hold values from -1.8 to 1.8
- guide_scale: float32 [1], replicated, may hold values from 3 to 7
Outputs:
- guided: float32 [1536, 64], P(('parts', 'seq')), parts along dimension 0
There are 2 independent parts, one for each index of `parts`. A program takes and returns all parts, laid end to end along the dimension named above; an argument that names none is the same for every part. Nothing has to cross between parts.
Inputs may be any that keep to these rules, and one draw needn't show every extreme that they name: `frame_counts`: latent frames of the 4 videos in packing order; they sum to 24 and the largest is exactly 16. `text_lengths`: live prompt tokens, counted from the front of each prompt.
All inputs are finite; a program needn't handle non-finite values.
Results may differ from a plain program's by a relative error of at most 0.0049.
Values may be sent and summed in bfloat16 or wider, within the bound.
A program may use at most 64 MiB of HBM per device.

v0:
```python
import jax
import jax.numpy as jnp
from jax import lax
from jax.sharding import PartitionSpec as P

HEAD_CHANNELS = 128
TPF = 32
TEXT = 256
VIDEOS = 4


def partner_2(value, axis, stride):
    mask = 2**stride
    pairs = [(source, source ^ mask) for source in range(lax.axis_size(axis))]
    return lax.ppermute(value, axis, pairs)


def local_attend(queries, incoming_keys, value_rows, allowed):
    logit_scores = jnp.einsum(
        "qd,kd->qk", queries, incoming_keys, preferred_element_type=jnp.float32
    ) * HEAD_CHANNELS ** (-0.5)
    logit_scores = jnp.where(allowed, logit_scores, -1e30)
    row_max = jnp.max(logit_scores, axis=-1, keepdims=True)
    raised = jnp.exp(logit_scores - row_max)
    softmax_weights = (raised / jnp.sum(raised, axis=-1, keepdims=True)).astype(jnp.bfloat16)
    return jnp.einsum("qk,kd->qd", softmax_weights, value_rows, preferred_element_type=jnp.float32)


def halve_rows(packed, devices):
    tok_dev, features = packed.shape
    head_count = features // HEAD_CHANNELS
    parted = packed.reshape(2, tok_dev // 2, head_count, HEAD_CHANNELS).transpose(2, 0, 1, 3)
    return parted.reshape(devices, tok_dev // 2, HEAD_CHANNELS)


def branch_sets(received, device_slices):
    row_count = received.shape[1]
    channels = received.shape[2]
    grouped = received.reshape(device_slices, 2, row_count, channels)
    return grouped.transpose(1, 0, 2, 3).reshape(2, device_slices * row_count, channels)


def local(
    queries,
    self_keys,
    self_values,
    residual_in,
    text_keys,
    text_values,
    text_lengths,
    frame_counts,
    mod_gain,
    mod_shift,
    head_weight,
    head_bias,
    guide_scale,
):
    devices = lax.axis_size("seq")
    parity = lax.axis_index("seq") % 2
    is_low = parity == 0
    tok_dev, features = queries.shape
    rows_half = tok_dev // 2
    head_count = features // HEAD_CHANNELS
    device_slices = devices // 2
    recv_query, recv_key, recv_value = (
        lax.all_to_all(
            halve_rows(queries, devices), "seq", split_axis=0, concat_axis=0, tiled=True
        ),
        lax.all_to_all(
            halve_rows(self_keys, devices), "seq", split_axis=0, concat_axis=0, tiled=True
        ),
        lax.all_to_all(
            halve_rows(self_values, devices), "seq", split_axis=0, concat_axis=0, tiled=True
        ),
    )
    own_pairs = jnp.concatenate([recv_key, recv_value], axis=-1)
    other_pairs = partner_2(own_pairs, "seq", 0)
    lower = jnp.where(is_low, own_pairs, other_pairs).reshape(
        device_slices, 2, rows_half, 2 * HEAD_CHANNELS
    )
    upper = jnp.where(is_low, other_pairs, own_pairs).reshape(
        device_slices, 2, rows_half, 2 * HEAD_CHANNELS
    )
    joined = jnp.stack([lower, upper], axis=2).reshape(device_slices, 2, tok_dev, 2 * HEAD_CHANNELS)
    pair_sets = joined.transpose(1, 0, 2, 3).reshape(2, device_slices * tok_dev, 2 * HEAD_CHANNELS)
    key_sets = pair_sets[..., :HEAD_CHANNELS]
    value_sets = pair_sets[..., HEAD_CHANNELS:]
    query_sets = branch_sets(recv_query, device_slices)
    half_dim = text_keys.shape[-1]
    partner = partner_2(jnp.concatenate([text_keys, text_values], axis=-1), "seq", 0)
    partner_keys = partner[..., :half_dim]
    partner_values = partner[..., half_dim:]
    cross_keys = jnp.where(
        is_low,
        jnp.concatenate([text_keys, partner_keys], -1),
        jnp.concatenate([partner_keys, text_keys], -1),
    )
    cross_values = jnp.where(
        is_low,
        jnp.concatenate([text_values, partner_values], -1),
        jnp.concatenate([partner_values, text_values], -1),
    )
    total_tokens = device_slices * tok_dev
    query_total = device_slices * rows_half
    all_frames = total_tokens // TPF
    most_frames = max(min(21, all_frames - 2 * VIDEOS), (all_frames + VIDEOS - 1) // VIDEOS + 1)
    key_window = min(total_tokens, most_frames * TPF)
    query_window = min(query_total, most_frames * TPF // 2 + rows_half)
    video_ends = jnp.cumsum(frame_counts) * TPF
    video_starts = video_ends - frame_counts * TPF
    key_places = jnp.arange(total_tokens, dtype=jnp.int32)
    key_videos = jnp.sum((key_places[:, None] >= video_ends[None, :]).astype(jnp.int32), axis=1)
    query_places = (
        jnp.arange(device_slices, dtype=jnp.int32)[:, None] * tok_dev
        + parity * rows_half
        + jnp.arange(rows_half, dtype=jnp.int32)[None, :]
    ).reshape(-1)
    query_videos = jnp.sum((query_places[:, None] >= video_ends[None, :]).astype(jnp.int32), axis=1)
    query_firsts = jnp.sum(
        (query_places[None, :] < video_starts[:, None]).astype(jnp.int32), axis=1
    )
    text_place = jnp.arange(TEXT, dtype=jnp.int32)

    def single_video(index, gathered):
        branch = index // VIDEOS
        video = index % VIDEOS
        query_start = jnp.clip(query_firsts[video], 0, query_total - query_window)
        key_start = jnp.clip(video_starts[video], 0, total_tokens - key_window)
        branch_queries = lax.dynamic_index_in_dim(query_sets, branch, 0, False)
        block_queries = lax.dynamic_slice_in_dim(branch_queries, query_start, query_window, 0)
        block_qvideos = lax.dynamic_slice_in_dim(query_videos, query_start, query_window, 0)
        keys_now = lax.dynamic_slice_in_dim(
            lax.dynamic_index_in_dim(key_sets, branch, 0, False), key_start, key_window, 0
        )
        values_now = lax.dynamic_slice_in_dim(
            lax.dynamic_index_in_dim(value_sets, branch, 0, False), key_start, key_window, 0
        )
        block_kvideos = lax.dynamic_slice_in_dim(key_videos, key_start, key_window, 0)
        key_live = block_kvideos == video
        self_part = local_attend(
            block_queries,
            keys_now,
            values_now,
            jnp.broadcast_to(key_live[None, :], (query_window, key_window)),
        )
        prompt_keys = cross_keys[branch, video]
        prompt_values = cross_values[branch, video]
        text_live = text_place < text_lengths[branch, video]
        cross_part = local_attend(
            block_queries,
            prompt_keys,
            prompt_values,
            jnp.broadcast_to(text_live[None, :], (query_window, TEXT)),
        )
        result = (self_part + cross_part).astype(jnp.bfloat16)
        branch_rows = lax.dynamic_index_in_dim(gathered, branch, 0, False)
        previous = lax.dynamic_slice_in_dim(branch_rows, query_start, query_window, 0)
        merged = jnp.where((block_qvideos == video)[:, None], result, previous)
        branch_rows = lax.dynamic_update_slice_in_dim(branch_rows, merged, query_start, 0)
        return lax.dynamic_update_index_in_dim(gathered, branch_rows, branch, 0)

    attended = lax.fori_loop(
        0, 2 * VIDEOS, single_video, jnp.zeros((2, query_total, HEAD_CHANNELS), jnp.bfloat16)
    )
    outgoing = (
        attended.reshape(2, device_slices, rows_half, HEAD_CHANNELS)
        .transpose(1, 0, 2, 3)
        .reshape(devices, rows_half, HEAD_CHANNELS)
    )
    returned = lax.all_to_all(outgoing, "seq", split_axis=0, concat_axis=0, tiled=True)
    attention = (
        returned.reshape(head_count, 2, rows_half, HEAD_CHANNELS)
        .transpose(1, 2, 0, 3)
        .reshape(tok_dev, features)
    )
    hidden = residual_in.astype(jnp.float32) + attention.astype(jnp.float32)
    row_mean = jnp.mean(hidden, axis=-1, keepdims=True)
    centred = hidden - row_mean
    row_var = jnp.mean(centred * centred, axis=-1, keepdims=True)
    normed = (centred * lax.rsqrt(row_var + 1e-06) * mod_gain + mod_shift).astype(jnp.bfloat16)
    velocity = jnp.dot(normed, head_weight, preferred_element_type=jnp.float32) + head_bias
    outgoing_rows = lax.dynamic_slice_in_dim(velocity, (1 - parity) * rows_half, rows_half, 0)
    arrived = partner_2(outgoing_rows, "seq", 0)
    own_rows = lax.dynamic_slice_in_dim(velocity, parity * rows_half, rows_half, 0)
    conditional = jnp.where(is_low, own_rows, arrived)
    unconditional = jnp.where(is_low, arrived, own_rows)
    return unconditional + guide_scale[0] * (conditional - unconditional)


def solution(mesh):
    return jax.shard_map(
        local,
        mesh=mesh,
        in_specs=(
            P(("parts", "seq"), None),
            P(("parts", "seq"), None),
            P(("parts", "seq"), None),
            P(("parts", "seq"), None),
            P(None, "parts", None, "seq"),
            P(None, "parts", None, "seq"),
            P(None, "parts"),
            P("parts"),
            P(),
            P(),
            P(),
            P(),
            P(),
        ),
        out_specs=P(("parts", "seq"), None),
        check_vma=False,
    )
```

profile of v0, /device:TPU:0, one launch (start us, length us, event | category | flops | bytes accessed | tf_op | source)
XLA Modules:
  0.0 114.1 jit_solution(16046620229366909343)
XLA Ops:
  0.0 1.0 copy.73
  1.0 0.7 copy.59
  1.7 7.5 %all-to-all-start.1 = ((bf16[16,48,128]{2,1,0:T(8,128)(2,1)}), bf16[16,48,128]{2,1,0:T(8,128)(2,1)S(1)}, u32[]{:S(2)}, u32[]{:S(2)}) async-start(bf16[16,48,128]{2,1,0:T(8,128)(2,1)} %bitcast.8), calls=%async_computation.1 | async-start | bytes 393216 | tf_op jit(solution)/shard_map/all_to_all | solution.py:69
  11.5 0.7 copy.60
  13.2 5.0 %all-to-all-done.1 = bf16[16,48,128]{2,1,0:T(8,128)(2,1)S(1)} async-done(((bf16[16,48,128]{2,1,0:T(8,128)(2,1)}), bf16[16,48,128]{2,1,0:T(8,128)(2,1)S(1)}, u32[]{:S(2)}, u32[]{:S(2)}) %all-to-all-start.1) | async-done | bytes 196640 | tf_op jit(solution)/shard_map/all_to_all | solution.py:69
  18.2 3.5 %all-to-all-start.2 = ((bf16[16,48,128]{2,1,0:T(8,128)(2,1)}), bf16[16,48,128]{2,1,0:T(8,128)(2,1)S(1)}, u32[]{:S(2)}, u32[]{:S(2)}) async-start(bf16[16,48,128]{2,1,0:T(8,128)(2,1)} %bitcast.10), calls=%async_computation.2 | async-start | bytes 393216 | tf_op jit(solution)/shard_map/all_to_all | solution.py:72
  21.9 0.7 copy.57
  22.7 8.0 %all-to-all-done.2 = bf16[16,48,128]{2,1,0:T(8,128)(2,1)S(1)} async-done(((bf16[16,48,128]{2,1,0:T(8,128)(2,1)}), bf16[16,48,128]{2,1,0:T(8,128)(2,1)S(1)}, u32[]{:S(2)}, u32[]{:S(2)}) %all-to-all-start.2) | async-done | bytes 196640 | tf_op jit(solution)/shard_map/all_to_all | solution.py:72
  30.7 3.5 %all-to-all-start = ((bf16[16,48,128]{2,1,0:T(8,128)(2,1)}), bf16[16,48,128]{2,1,0:T(8,128)(2,1)S(1)}, u32[]{:S(2)}, u32[]{:S(2)}) async-start(bf16[16,48,128]{2,1,0:T(8,128)(2,1)} %bitcast.3), calls=%async_computation | async-start | bytes 393216 | tf_op jit(solution)/shard_map/all_to_all | solution.py:66
  35.0 8.2 %all-to-all-done = bf16[16,48,128]{2,1,0:T(8,128)(2,1)S(1)} async-done(((bf16[16,48,128]{2,1,0:T(8,128)(2,1)}), bf16[16,48,128]{2,1,0:T(8,128)(2,1)S(1)}, u32[]{:S(2)}, u32[]{:S(2)}) %all-to-all-start) | async-done | bytes 196640 | tf_op jit(solution)/shard_map/all_to_all | solution.py:66
  43.4 1.2 %maximum_select_fusion = (bf16[2,4,256,128]{3,2,1,0:T(8,128)(2,1)S(1)}, bf16[2,4,256,128]{3,2,1,0:T(8,128)(2,1)S(1)}) fusion(bf16[2,4,256,64]{3,2,1,0:T(8,128)(2,1)S(1)} %get-tuple-element.424, bf16[2,4,256,64]{3,2,1,0:T(8,128)(2,1)S(1)} %copy.65, pred[]{:T(512)S(6)} %eq.57, bf16[2,4,256,64]{3,2,1,0:T(8,128)(2,1)S(1)} %copy.64, ...), kind=kLoop, calls=%fused_computation.37 | loop fusion | flops 4718592 | bytes 2097153 | tf_op jit(solution)/shard_map/jit(_where)/select_n | solution.py:93
  44.6 1.1 broadcast_select_fusion.1
  46.7 49.9 %while.17 = (s32[]{:T(128)}, bf16[2,384,128]{2,1,0:T(8,128)(2,1)S(1)}, s32[4]{0:T(128)S(1)}, s32[384]{0:T(512)S(1)}, s32[4]{0:T(128)S(1)}, /*index=5*/s32[768]{0...) while((s32[]{:T(128)}, ...), condition=%wide.region_9.10_spmd.clone, body=%wide.region_4.9_spmd.clone.sunk | while | flops 121522056 | bytes 3999144 | solution.py:162
  53.0 0.7 dynamic_slice.202
  59.3 0.7 dynamic_slice.202
  65.5 0.7 dynamic_slice.202
  71.7 0.7 dynamic_slice.202
  78.0 0.7 dynamic_slice.202
  84.2 0.7 dynamic_slice.202
  96.6 0.7 copy.69
  97.3 3.5 %all-to-all-start.3 = ((bf16[16,48,128]{2,1,0:T(8,128)(2,1)}), bf16[16,48,128]{2,1,0:T(8,128)(2,1)S(1)}, u32[]{:S(2)}, u32[]{:S(2)}) async-start(bf16[16,48,128]{2,1,0:T(8,128)(2,1)} %bitcast.18), calls=%async_computation.3 | async-start | bytes 393216 | tf_op jit(solution)/shard_map/all_to_all | solution.py:170
  100.8 8.9 %all-to-all-done.3 = bf16[16,48,128]{2,1,0:T(8,128)(2,1)S(1)} async-done(((bf16[16,48,128]{2,1,0:T(8,128)(2,1)}), bf16[16,48,128]{2,1,0:T(8,128)(2,1)S(1)}, u32[]{:S(2)}, u32[]{:S(2)}) %all-to-all-start.3) | async-done | bytes 196640 | tf_op jit(solution)/shard_map/all_to_all | solution.py:170
  110.0 0.7 copy-done.1
  113.4 0.7 copy.71
  (160 shorter events, 41.7 us)
Async XLA Ops:
  0.0 111.1 %copy-start = (bf16[1024,64]{0,1:T(8,128)(2,1)S(1)}, bf16[1024,64]{0,1:T(8,128)(2,1)}, u32[]{:S(2)}) copy-start(bf16[1024,64]{0,1:T(8,128)(2,1)} %param.25) | copy-start | bytes 393220
  1.7 7.6 %copy-start.2 = (bf16[2,4,256,64]{2,3,1,0:T(8,128)(2,1)S(1)}, bf16[2,4,256,64]{2,3,1,0:T(8,128)(2,1)}, u32[]{:S(2)}) copy-start(bf16[2,4,256,64]{2,3,1,0:T(8,128)(2,1)} %param.20) | copy-start | bytes 786436
  1.7 16.5 %all-to-all-start.1 = ((bf16[16,48,128]{2,1,0:T(8,128)(2,1)}), bf16[16,48,128]{2,1,0:T(8,128)(2,1)S(1)}, u32[]{:S(2)}, u32[]{:S(2)}) async-start(bf16[16,48,128]{2,1,0:T(8,128)(2,1)} %bitcast.8), calls=%async_computation.1 | async-start | bytes 393216 | tf_op jit(solution)/shard_map/all_to_all | solution.py:69
  9.3 1.0 copy-start.3
  10.5 0.9 copy-start.4
  10.8 32.3 %collective-permute-start.1 = (bf16[2,4,256,128]{3,2,1,0:T(8,128)(2,1)S(1)}, bf16[2,4,256,128]{3,2,1,0:T(8,128)(2,1)S(1)}, u32[]{:S(2)}, u32[]{:S(2)}) collective-permute-start(bf16[2,4,256,128]{3,2,1,0:T(8,128)(2,1)S(1)} %pad_maximum_fusion.1), channel_id=1, source_target_pairs={{0,1},{1,0},{2,3},{3,2},{4,5},{5,4},{6,7},{7,6},{8,9},{9,8},{10,11... | collective-permute-start | bytes 1572872 | tf_op jit(solution)/shard_map/ppermute | solution.py:15
  11.5 1.6 %copy-start.5 = (bf16[96,1024]{1,0:T(8,128)(2,1)S(1)}, bf16[96,1024]{1,0:T(8,128)(2,1)}, u32[]{:S(2)}) copy-start(bf16[96,1024]{1,0:T(8,128)(2,1)} %param.15) | copy-start | bytes 589828
  12.2 0.7 copy-start.9
  18.2 12.5 %all-to-all-start.2 = ((bf16[16,48,128]{2,1,0:T(8,128)(2,1)}), bf16[16,48,128]{2,1,0:T(8,128)(2,1)S(1)}, u32[]{:S(2)}, u32[]{:S(2)}) async-start(bf16[16,48,128]{2,1,0:T(8,128)(2,1)} %bitcast.10), calls=%async_computation.2 | async-start | bytes 393216 | tf_op jit(solution)/shard_map/all_to_all | solution.py:72
  30.7 12.5 %all-to-all-start = ((bf16[16,48,128]{2,1,0:T(8,128)(2,1)}), bf16[16,48,128]{2,1,0:T(8,128)(2,1)S(1)}, u32[]{:S(2)}, u32[]{:S(2)}) async-start(bf16[16,48,128]{2,1,0:T(8,128)(2,1)} %bitcast.3), calls=%async_computation | async-start | bytes 393216 | tf_op jit(solution)/shard_map/all_to_all | solution.py:66
  34.6 10.0 %collective-permute-start = (bf16[16,48,256]{2,1,0:T(8,128)(2,1)S(1)}, bf16[16,48,256]{2,1,0:T(8,128)(2,1)}, u32[]{:S(2)}, u32[]{:S(2)}) collective-permute-start(bf16[16,48,256]{2,1,0:T(8,128)(2,1)S(1)} %constant_dynamic-update-slice_fusion), channel_id=1, source_target_pairs={{0,1},{1,0},{2,3},{3,2},{4,5},{5,4},{6,7},{7,6},{8,9},{9,8},{10,11... | collective-permute-start | bytes 1179656 | tf_op jit(solution)/shard_map/ppermute | solution.py:15
  46.0 0.7 copy-start.6
  97.3 12.5 %all-to-all-start.3 = ((bf16[16,48,128]{2,1,0:T(8,128)(2,1)}), bf16[16,48,128]{2,1,0:T(8,128)(2,1)S(1)}, u32[]{:S(2)}, u32[]{:S(2)}) async-start(bf16[16,48,128]{2,1,0:T(8,128)(2,1)} %bitcast.18), calls=%async_computation.3 | async-start | bytes 393216 | tf_op jit(solution)/shard_map/all_to_all | solution.py:170
  109.8 0.9 copy-start.1
  110.9 0.7 copy-start.7
  110.9 0.7 copy-start.8
  111.1 0.7 copy-start.10
  112.1 1.2 %collective-permute-start.2 = (f32[48,64]{0,1:T(8,128)S(1)}, f32[48,64]{0,1:T(8,128)S(1)}, u32[]{:S(2)}, u32[]{:S(2)}) collective-permute-start(f32[48,64]{0,1:T(8,128)S(1)} %constant_dynamic-slice_fusion), channel_id=1, source_target_pairs={{0,1},{1,0},{2,3},{3,2},{4,5},{5,4},{6,7},{7,6},{8,9},{9,8},{10,11... | collective-permute-start | bytes 36872 | tf_op jit(solution)/shard_map/ppermute | solution.py:15
where the time goes:
time: 115 us; the launch traced here: 114 us
  waiting for transfers between devices  30.8 us (27%)
  local copies, waits for them, and re-layouts  27.7 us (24%)
  starting transfers between devices  18.9 us (16%)
  other arithmetic  13.5 us (12%)
  loops' own time  11.8 us (10%)
  matrix products  10.4 us (9%)
    another operation x1, loops' own time, local(): lax.fori_loop(0, 2 * VIDEOS, single_video, jnp.zeros((2, query_total, HEA...  11.8 us
    all_to_all x1, waiting for transfers between devices, local(): lax.all_to_all(outgoing, 'seq', split_axis=0, concat_axis=0, tiled=True)  8.92 us
    all_to_all x1, waiting for transfers between devices, local(): lax.all_to_all(halve_rows(queries, devices), 'seq', split_axis=0, concat_...  8.2 us
    all_to_all x1, waiting for transfers between devices, local(): lax.all_to_all(halve_rows(self_values, devices), 'seq', split_axis=0, con...  8.05 us
    all_to_all x1, starting transfers between devices, local(): lax.all_to_all(halve_rows(self_keys, devices), 'seq', split_axis=0, conca...  7.55 us
    dot_general x16, matrix products, local_attend(): jnp.einsum('qd,kd->qk', queries, incoming_keys, preferred_element_type=jn...  5.37 us
    dynamic_slice x8, local copies, waits for them, and re-layouts, single_video(): key_start = jnp.clip(video_starts[video], 0, total_tokens - key_window)  5.33 us
    dynamic_slice x8, local copies, waits for them, and re-layouts, single_video(): query_start = jnp.clip(query_firsts[video], 0, query_total - query_window)  5.3 us
  transfers between devices with their start and end apart: 7, of which 5 were waited for; matrix products, arithmetic and copies ran while one was open for 4% of the time, Pallas kernels for 0%

commit v1 on v0

v1 whole, which is shorter than its diff:
```python
import functools
import math

import jax
import jax.numpy as jnp
from jax import lax
from jax.experimental import pallas as pl
from jax.experimental.pallas import tpu as pltpu
from jax.sharding import PartitionSpec as P

HEAD_CHANNELS = 128
TPF = 32
PENALTY = -1e30
EXP_SCALE = HEAD_CHANNELS ** (-0.5) * math.log2(math.e)
MESH_ID = pl.DeviceIdType.MESH


def inside(rows, starts, ends):
    lane = lax.broadcasted_iota(jnp.int32, (1, HEAD_CHANNELS), 1)
    low = jnp.zeros((1, HEAD_CHANNELS), jnp.int32)
    high = jnp.zeros((1, HEAD_CHANNELS), jnp.int32)
    for f, (start, end) in enumerate(zip(starts, ends)):
        low = jnp.where(lane == f, start, low)
        high = jnp.where(lane == f, end, high)
    row = lax.broadcasted_iota(jnp.int32, (rows, HEAD_CHANNELS), 0)
    return (row >= low) & (row < high)


def weights_of(queries, keys):
    scores = lax.dot_general(
        queries, keys, (((1,), (1,)), ((), ())), preferred_element_type=jnp.float32
    )
    top = jnp.max(scores, axis=-1, keepdims=True)
    raised = jnp.exp2((scores - top) * EXP_SCALE)
    total = jnp.sum(raised, axis=-1, keepdims=True)
    return (raised * (1.0 / total)).astype(jnp.bfloat16)


def kernel(
    n,
    q_ref,
    k_ref,
    v_ref,
    x_ref,
    tk_ref,
    tv_ref,
    lengths_ref,
    frames_ref,
    gain_ref,
    shift_ref,
    weight_ref,
    bias_ref,
    out_ref,
    qb,
    kb,
    vb,
    q_hot,
    k_pen,
    tkb,
    tvb,
    t_keys,
    t_vals,
    p_self,
    cross,
    ob,
    att,
    xb,
    qkv_send,
    qkv_recv,
    pair_send,
    pair_recv,
    out_send,
    out_recv,
    here_sem,
):
    me = lax.axis_index("seq")
    chips = n // 2
    chip, core = me // 2, me % 2
    partner = chip * 2 + (1 - core)
    rows = q_ref.shape[0]
    half = rows // 2
    tokens = chips * rows
    videos = frames_ref.shape[0]
    slots = tk_ref.shape[1]
    text = slots // videos
    sources = (q_ref, k_ref, v_ref)
    landings = (qb, kb, vb)

    def block(index, size):
        return pl.ds(pl.multiple_of(index * size, size), size)

    def qkv_copy(which, peer):
        return pltpu.make_async_remote_copy(
            src_ref=sources[which].at[:, block(peer, HEAD_CHANNELS)],
            dst_ref=landings[which].at[block(chip, rows)],
            send_sem=qkv_send.at[which, peer],
            recv_sem=qkv_recv.at[which, chip],
            device_id={"seq": peer * 2 + core},
            device_id_type=MESH_ID,
        )

    def own_copy(which):
        return pltpu.make_async_copy(
            sources[which].at[:, block(chip, HEAD_CHANNELS)],
            landings[which].at[block(chip, rows)],
            qkv_recv.at[which, chip],
        )

    def qkv_wait(which, peer):
        place = landings[which].at[block(peer, rows)]
        pltpu.make_async_copy(place, place, qkv_recv.at[which, peer]).wait()

    pair_parts = (
        (tk_ref.at[1 - core], tkb.at[core]),
        (tv_ref.at[1 - core], tvb.at[core]),
        (x_ref.at[block(1 - core, half)], xb.at[core]),
    )
    here_parts = (
        (tk_ref.at[core], tkb.at[core]),
        (tv_ref.at[core], tvb.at[core]),
        (x_ref.at[block(core, half)], xb.at[core]),
    )
    pair_copies = [
        pltpu.make_async_remote_copy(
            src_ref=source,
            dst_ref=landing,
            send_sem=pair_send.at[i],
            recv_sem=pair_recv.at[i],
            device_id={"seq": partner},
            device_id_type=MESH_ID,
        )
        for i, (source, landing) in enumerate(pair_parts)
    ]
    here_copies = [
        pltpu.make_async_copy(source, landing, here_sem.at[i])
        for i, (source, landing) in enumerate(here_parts)
    ]

    barrier = pltpu.get_barrier_semaphore()

    @pl.loop(1, n)
    def _(step):
        pl.semaphore_signal(
            barrier, inc=1, device_id={"seq": lax.rem(me + step, n)}, device_id_type=MESH_ID
        )

    for copy in here_copies:
        copy.start()
    for which in range(3):
        own_copy(which).start()

    pl.semaphore_wait(barrier, n - 1)

    pair_copies[0].start()
    for which in range(3):

        @pl.loop(1, chips)
        def _(step, which=which):
            qkv_copy(which, lax.rem(chip + step, chips)).start()

        if which < 2:
            pair_copies[which + 1].start()

    starts, ends, position = [], [], jnp.int32(0)
    for f in range(videos):
        starts.append(position)
        position = position + frames_ref[f] * TPF
        ends.append(position)
    same = inside(tokens, starts, ends)
    q_hot[...] = jnp.where(same, 1.0, 0.0).astype(jnp.bfloat16)
    k_pen[...] = jnp.where(same, 0.0, PENALTY).astype(jnp.bfloat16)
    lengths = [
        jnp.where(core == 0, lengths_ref[0, f], lengths_ref[1, f]) for f in range(videos)
    ]
    live = inside(
        slots, [f * text for f in range(videos)], [f * text + lengths[f] for f in range(videos)]
    )
    t_keys[:, HEAD_CHANNELS:] = jnp.where(live, 0.0, PENALTY).astype(jnp.bfloat16)

    def pair_wait(i):
        here_copies[i].wait()
        pair_copies[i].wait_recv()

    pair_wait(0)
    t_keys[:, :HEAD_CHANNELS] = jnp.concatenate([tkb[0], tkb[1]], axis=-1)
    pair_wait(1)
    t_vals[...] = jnp.concatenate([tvb[0], tvb[1]], axis=-1)

    def query_block(index):
        place = block(index, rows)
        return jnp.concatenate([qb[place, :], q_hot[place, :]], axis=-1)

    @pl.loop(0, chips)
    def _(step):
        index = lax.rem(chip + step, chips)
        qkv_wait(0, index)
        weights = weights_of(query_block(index), t_keys[...])
        cross[block(index, rows), :] = jnp.dot(
            weights, t_vals[...], preferred_element_type=jnp.float32
        )

    @pl.loop(0, chips)
    def _(step):
        qkv_wait(1, step)

    @pl.loop(0, chips)
    def _(step):
        index = lax.rem(chip + step, chips)
        keys = jnp.concatenate([kb[...], k_pen[...]], axis=-1)
        p_self[block(index, rows), :] = weights_of(query_block(index), keys)

    @pl.loop(0, chips)
    def _(step):
        qkv_wait(2, step)

    def out_copy(device):
        return pltpu.make_async_remote_copy(
            src_ref=ob.at[block(device, half)],
            dst_ref=att.at[core, :, block(chip, HEAD_CHANNELS)],
            send_sem=out_send.at[device],
            recv_sem=out_recv.at[me],
            device_id={"seq": device},
            device_id_type=MESH_ID,
        )

    def out_own():
        return pltpu.make_async_copy(
            ob.at[block(me, half)],
            att.at[core, :, block(chip, HEAD_CHANNELS)],
            out_recv.at[me],
        )

    @pl.loop(0, chips)
    def _(step):
        index = lax.rem(chip + 1 + step, chips)
        place = block(index, rows)
        mixed = cross[place, :] + jnp.dot(
            p_self[place, :], vb[...], preferred_element_type=jnp.float32
        )
        ob[place, :] = mixed.astype(jnp.bfloat16)
        for side in range(2):
            device = index * 2 + side

            @pl.when(device != me)
            def _():
                out_copy(device).start()

            @pl.when(device == me)
            def _():
                out_own().start()

    pair_wait(2)

    @pl.loop(0, n)
    def _(device):
        place = att.at[device % 2, :, block(device // 2, HEAD_CHANNELS)]
        pltpu.make_async_copy(place, place, out_recv.at[device]).wait()

    features = x_ref.shape[1]
    hidden = (xb[...].astype(jnp.float32) + att[...].astype(jnp.float32)).reshape(rows, features)
    centred = hidden - jnp.mean(hidden, axis=-1, keepdims=True)
    spread = jnp.mean(centred * centred, axis=-1, keepdims=True)
    normed = centred * lax.rsqrt(spread + 1e-06) * gain_ref[...] + shift_ref[...]
    velocity = (
        jnp.dot(normed.astype(jnp.bfloat16), weight_ref[...], preferred_element_type=jnp.float32)
        + bias_ref[...]
    )
    out_ref[...] = velocity

    for copy in pair_copies:
        copy.wait_send()
    for which in range(3):

        @pl.loop(1, chips)
        def _(step, which=which):
            qkv_copy(which, lax.rem(chip + step, chips)).wait_send()

    @pl.loop(1, n)
    def _(step):
        out_copy(lax.rem(me + step, n)).wait_send()


def local(
    queries,
    self_keys,
    self_values,
    residual_in,
    text_keys,
    text_values,
    text_lengths,
    frame_counts,
    mod_gain,
    mod_shift,
    head_weight,
    head_bias,
    guide_scale,
):
    n = lax.axis_size("seq")
    chips = n // 2
    rows, features = queries.shape
    half = rows // 2
    outs = head_weight.shape[1]
    tokens = chips * rows
    branches, videos, text, share = text_keys.shape
    slots = videos * text
    bf16, f32 = jnp.bfloat16, jnp.float32
    anywhere = pl.BlockSpec(memory_space=pl.ANY)
    scalar = pl.BlockSpec(memory_space=pltpu.SMEM)
    vector = pl.BlockSpec(memory_space=pltpu.VMEM)
    velocity = pl.pallas_call(
        functools.partial(kernel, n),
        out_shape=jax.ShapeDtypeStruct((rows, outs), f32),
        in_specs=[anywhere] * 6 + [scalar] * 2 + [vector] * 4,
        out_specs=vector,
        scratch_shapes=[
            pltpu.VMEM((tokens, HEAD_CHANNELS), bf16),
            pltpu.VMEM((tokens, HEAD_CHANNELS), bf16),
            pltpu.VMEM((tokens, HEAD_CHANNELS), bf16),
            pltpu.VMEM((tokens, HEAD_CHANNELS), bf16),
            pltpu.VMEM((tokens, HEAD_CHANNELS), bf16),
            pltpu.VMEM((2, slots, share), bf16),
            pltpu.VMEM((2, slots, share), bf16),
            pltpu.VMEM((slots, 2 * HEAD_CHANNELS), bf16),
            pltpu.VMEM((slots, HEAD_CHANNELS), bf16),
            pltpu.VMEM((tokens, tokens), bf16),
            pltpu.VMEM((tokens, HEAD_CHANNELS), f32),
            pltpu.VMEM((tokens, HEAD_CHANNELS), bf16),
            pltpu.VMEM((2, half, features), bf16),
            pltpu.VMEM((2, half, features), bf16),
            pltpu.SemaphoreType.DMA((3, chips)),
            pltpu.SemaphoreType.DMA((3, chips)),
            pltpu.SemaphoreType.DMA((3,)),
            pltpu.SemaphoreType.DMA((3,)),
            pltpu.SemaphoreType.DMA((n,)),
            pltpu.SemaphoreType.DMA((n,)),
            pltpu.SemaphoreType.DMA((3,)),
        ],
        compiler_params=pltpu.CompilerParams(
            collective_id=0, has_side_effects=True, vmem_limit_bytes=60 * 1024 * 1024
        ),
        name="guided_block",
    )(
        queries,
        self_keys,
        self_values,
        residual_in,
        text_keys.reshape(branches, slots, share),
        text_values.reshape(branches, slots, share),
        text_lengths,
        frame_counts,
        mod_gain.reshape(1, features),
        mod_shift.reshape(1, features),
        head_weight,
        head_bias.reshape(1, outs),
    )
    conditional, unconditional = velocity[:half], velocity[half:]
    return unconditional + guide_scale[0] * (conditional - unconditional)


def solution(mesh):
    return jax.shard_map(
        local,
        mesh=mesh,
        in_specs=(
            P(("parts", "seq"), None),
            P(("parts", "seq"), None),
            P(("parts", "seq"), None),
            P(("parts", "seq"), None),
            P(None, "parts", None, "seq"),
            P(None, "parts", None, "seq"),
            P(None, "parts"),
            P("parts"),
            P(),
            P(),
            P(),
            P(),
            P(),
        ),
        out_specs=P(("parts", "seq"), None),
        check_vma=False,
    )
```

time: 115 us -> 38.1 us (0.33)
  Pallas kernels: 0 us -> 32 us
  waiting for transfers between devices: 30.8 us -> 0 us
  local copies, waits for them, and re-layouts: 27.7 us -> 3.85 us
  starting transfers between devices: 18.9 us -> 0 us
  other arithmetic: 13.5 us -> 1.37 us
  loops' own time: 11.8 us -> 0 us
  matrix products: 10.4 us -> 0 us
    pallas_call x0 -> x1, Pallas kernels: none -> 32 us  [local(): pl.pallas_call(functools.partial(kernel, n), out_shape=jax.ShapeDtypeStru...]
    all_to_all x4 -> x0, waiting for transfers between devices: 30.2 us -> none  [the longest x1 8.92 us: local(): lax.all_to_all(outgoing, 'seq', split_axis=0, concat_axis=0, tiled=True)]
    all_to_all x4 -> x0, starting transfers between devices: 18.1 us -> none  [the longest x1 7.55 us: local(): lax.all_to_all(halve_rows(self_keys, devices), 'seq', split_axis=0, conca...]
    dynamic_slice x25 -> x0, local copies, waits for them, and re-layouts: 15.4 us -> none  [the longest x8 5.33 us: single_video(): key_start = jnp.clip(video_starts[video], 0, total_tokens - key_window)]
    another operation x1 -> x0, loops' own time: 11.8 us -> none  [local(): lax.fori_loop(0, 2 * VIDEOS, single_video, jnp.zeros((2, query_total, HEA...]
    dot_general x33 -> x0, matrix products: 10.4 us -> none  [the longest x16 5.37 us: local_attend(): jnp.einsum('qd,kd->qk', queries, incoming_keys, preferred_element_type=jn...]
    reduce_sum x21 -> x0, other arithmetic: 4.77 us -> none  [the longest x16 4.06 us: local_attend(): jnp.sum(raised, axis=-1, keepdims=True)]
    lt x8 -> x0, other arithmetic: 4.5 us -> none  [single_video(): text_live = text_place < text_lengths[branch, video]]
  transfers between devices with their start and end apart: 7 -> 0, of which waited for: 5 -> 0; matrix products, arithmetic and copies ran while one was open for 4% -> 0% of each run, Pallas kernels for 0% -> 0%
where the time goes in v1:
time: 38.1 us; the launch traced here: 37.9 us
  Pallas kernels  32 us (84%)
  local copies, waits for them, and re-layouts  3.85 us (10%)
  other arithmetic  1.37 us (4%)
  between operations  0.66 us (2%)
    pallas_call x1, Pallas kernels, local(): pl.pallas_call(functools.partial(kernel, n), out_shape=jax.ShapeDtypeStru...  32 us
    unnamed x7, local copies, waits for them, and re-layouts  3.85 us
    add x1, other arithmetic, local(): return unconditional + guide_scale[0] * (conditional - unconditional)  1.37 us

profile of v1, /device:TPU:0, one launch (start us, length us, event | category | flops | bytes accessed | tf_op | source)
XLA Modules:
  0.0 37.9 jit_solution(5962782537356738725)
XLA Ops:
  0.0 0.0 copy-start
  0.0 2.0 %copy.14 = bf16[2,4,256,64]{3,2,1,0:T(8,128)(2,1)} copy(bf16[2,4,256,64]{2,3,1,0:T(8,128)(2,1)} %param.17) | data formatting | bytes 524288 | tf_op args[4]
  2.0 0.0 copy-done
  2.0 0.0 copy-start.1
  2.0 1.0 %copy.15 = bf16[2,4,256,64]{3,2,1,0:T(8,128)(2,1)} copy(bf16[2,4,256,64]{2,3,1,0:T(8,128)(2,1)S(1)} %copy-done) | data formatting | bytes 524288 | tf_op args[5]
  3.0 0.0 copy-done.1
  3.0 0.9 %copy.16.weight_ref = bf16[1024,64]{1,0:T(8,128)(2,1)} copy(bf16[1024,64]{0,1:T(8,128)(2,1)S(1)} %copy-done.1) | data formatting | bytes 262144 | tf_op args[10]
  3.8 32.0 %guided_block.1 = f32[96,64]{1,0:T(8,128)} custom-call(bf16[96,1024]{1,0:T(8,128)(2,1)} %q_ref.1, bf16[96,1024]{1,0:T(8,128)(2,1)} %k_ref.1, bf16[96,1024]{1,0:T(8,128)(2,1)} %v_ref.1, bf16[96,1024]{1,0:T(8,128)(2,1)} %x_ref.1, bf16[2,1024,64]{2,1,0:T(8,128)(2,1)} %bitcast.7, bf16[2,1024,64]{2,1,0:T(8,128)(2,1)} %bitcast.8, s32[2,4]{1,0:T(2,128)} %lengths_ref.1, ...), custom_call_target="tpu_custom_call" | custom-call | tf_op jit(solution)/shard_map/guided_block/pallas_call | solution.py:310
  36.5 1.4 %multiply_add_fusion = f32[48,64]{1,0:T(8,128)} fusion(f32[96,64]{1,0:T(8,128)} %guided_block.1, f32[]{:T(128)} %bitcast.6), kind=kLoop, calls=%fused_computation | loop fusion | flops 9216 | bytes 36868 | tf_op jit(solution)/shard_map/add | solution.py:357
Async XLA Ops:
  0.0 2.0 %copy-start = (bf16[2,4,256,64]{2,3,1,0:T(8,128)(2,1)S(1)}, bf16[2,4,256,64]{2,3,1,0:T(8,128)(2,1)}, u32[]{:S(2)}) copy-start(bf16[2,4,256,64]{2,3,1,0:T(8,128)(2,1)} %param.18) | copy-start | bytes 786436
  2.0 1.0 %copy-start.1 = (bf16[1024,64]{0,1:T(8,128)(2,1)S(1)}, bf16[1024,64]{0,1:T(8,128)(2,1)}, u32[]{:S(2)}) copy-start(bf16[1024,64]{0,1:T(8,128)(2,1)} %param.23) | copy-start | bytes 393220

commit v2 on v1

--- a/solution.py
+++ b/solution.py
@@ -15,21 +15,19 @@
 MESH_ID = pl.DeviceIdType.MESH
 
 
-def inside(rows, starts, ends):
-    lane = lax.broadcasted_iota(jnp.int32, (1, HEAD_CHANNELS), 1)
-    low = jnp.zeros((1, HEAD_CHANNELS), jnp.int32)
-    high = jnp.zeros((1, HEAD_CHANNELS), jnp.int32)
+def inside(shape, dim, starts, ends):
+    thin = tuple(1 if i == dim else size for i, size in enumerate(shape))
+    feature = lax.broadcasted_iota(jnp.int32, thin, 1 - dim)
+    low = jnp.zeros(thin, jnp.int32)
+    high = jnp.zeros(thin, jnp.int32)
     for f, (start, end) in enumerate(zip(starts, ends)):
-        low = jnp.where(lane == f, start, low)
-        high = jnp.where(lane == f, end, high)
-    row = lax.broadcasted_iota(jnp.int32, (rows, HEAD_CHANNELS), 0)
-    return (row >= low) & (row < high)
-
-
-def weights_of(queries, keys):
-    scores = lax.dot_general(
-        queries, keys, (((1,), (1,)), ((), ())), preferred_element_type=jnp.float32
-    )
+        low = jnp.where(feature == f, start, low)
+        high = jnp.where(feature == f, end, high)
+    place = lax.broadcasted_iota(jnp.int32, shape, dim)
+    return (place >= low) & (place < high)
+
+
+def weights_of(scores):
     top = jnp.max(scores, axis=-1, keepdims=True)
     raised = jnp.exp2((scores - top) * EXP_SCALE)
     total = jnp.sum(raised, axis=-1, keepdims=True)
@@ -50,15 +48,15 @@
     shift_ref,
     weight_ref,
     bias_ref,
+    guide_ref,
     out_ref,
     qb,
     kb,
     vb,
     q_hot,
-    k_pen,
-    tkb,
-    tvb,
+    keys,
     t_keys,
+    t_vals_in,
     t_vals,
     p_self,
     cross,
@@ -81,8 +79,7 @@
     half = rows // 2
     tokens = chips * rows
     videos = frames_ref.shape[0]
-    slots = tk_ref.shape[1]
-    text = slots // videos
+    share, text = tk_ref.shape[2:]
     sources = (q_ref, k_ref, v_ref)
     landings = (qb, kb, vb)
 
@@ -110,14 +107,16 @@
         place = landings[which].at[block(peer, rows)]
         pltpu.make_async_copy(place, place, qkv_recv.at[which, peer]).wait()
 
+    key_place = t_keys.at[:, block(core, share), :]
+    value_place = t_vals_in.at[:, block(core, share), :]
     pair_parts = (
-        (tk_ref.at[1 - core], tkb.at[core]),
-        (tv_ref.at[1 - core], tvb.at[core]),
+        (tk_ref.at[1 - core], key_place),
+        (tv_ref.at[1 - core], value_place),
         (x_ref.at[block(1 - core, half)], xb.at[core]),
     )
     here_parts = (
-        (tk_ref.at[core], tkb.at[core]),
-        (tv_ref.at[core], tvb.at[core]),
+        (tk_ref.at[core], key_place),
+        (tv_ref.at[core], value_place),
         (x_ref.at[block(core, half)], xb.at[core]),
     )
     pair_copies = [
@@ -166,25 +165,28 @@
         starts.append(position)
         position = position + frames_ref[f] * TPF
         ends.append(position)
-    same = inside(tokens, starts, ends)
+    same = inside((tokens, HEAD_CHANNELS), 0, starts, ends)
     q_hot[...] = jnp.where(same, 1.0, 0.0).astype(jnp.bfloat16)
-    k_pen[...] = jnp.where(same, 0.0, PENALTY).astype(jnp.bfloat16)
-    lengths = [
-        jnp.where(core == 0, lengths_ref[0, f], lengths_ref[1, f]) for f in range(videos)
-    ]
-    live = inside(
-        slots, [f * text for f in range(videos)], [f * text + lengths[f] for f in range(videos)]
-    )
-    t_keys[:, HEAD_CHANNELS:] = jnp.where(live, 0.0, PENALTY).astype(jnp.bfloat16)
+    apart = ~inside((HEAD_CHANNELS, tokens), 1, starts, ends)
+    keys[HEAD_CHANNELS:, :] = jnp.where(apart, PENALTY, 0.0).astype(jnp.bfloat16)
+    for f in range(videos):
+        length = jnp.where(core == 0, lengths_ref[0, f], lengths_ref[1, f])
+        live = inside(
+            (HEAD_CHANNELS, text),
+            1,
+            [0] * videos,
+            [length if other == f else 0 for other in range(videos)],
+        )
+        t_keys[f, HEAD_CHANNELS:, :] = jnp.where(live, 0.0, PENALTY).astype(jnp.bfloat16)
 
     def pair_wait(i):
         here_copies[i].wait()
         pair_copies[i].wait_recv()
 
     pair_wait(0)
-    t_keys[:, :HEAD_CHANNELS] = jnp.concatenate([tkb[0], tkb[1]], axis=-1)
     pair_wait(1)
-    t_vals[...] = jnp.concatenate([tvb[0], tvb[1]], axis=-1)
+    for f in range(videos):
+        t_vals[f * text : (f + 1) * text, :] = t_vals_in[f].T
 
     def query_block(index):
         place = block(index, rows)
@@ -194,7 +196,15 @@
     def _(step):
         index = lax.rem(chip + step, chips)
         qkv_wait(0, index)
-        weights = weights_of(query_block(index), t_keys[...])
+        queries = query_block(index)
+        scores = jnp.concatenate(
+            [
+                jnp.dot(queries, t_keys[f], preferred_element_type=jnp.float32)
+                for f in range(videos)
+            ],
+            axis=-1,
+        )
+        weights = weights_of(scores)
         cross[block(index, rows), :] = jnp.dot(
             weights, t_vals[...], preferred_element_type=jnp.float32
         )
@@ -203,11 +213,13 @@
     def _(step):
         qkv_wait(1, step)
 
+    keys[:HEAD_CHANNELS, :] = kb[...].T
+
     @pl.loop(0, chips)
     def _(step):
         index = lax.rem(chip + step, chips)
-        keys = jnp.concatenate([kb[...], k_pen[...]], axis=-1)
-        p_self[block(index, rows), :] = weights_of(query_block(index), keys)
+        scores = jnp.dot(query_block(index), keys[...], preferred_element_type=jnp.float32)
+        p_self[block(index, rows), :] = weights_of(scores)
 
     @pl.loop(0, chips)
     def _(step):
@@ -262,10 +274,16 @@
     spread = jnp.mean(centred * centred, axis=-1, keepdims=True)
     normed = centred * lax.rsqrt(spread + 1e-06) * gain_ref[...] + shift_ref[...]
     velocity = (
-        jnp.dot(normed.astype(jnp.bfloat16), weight_ref[...], preferred_element_type=jnp.float32)
+        lax.dot_general(
+            normed.astype(jnp.bfloat16),
+            weight_ref[...],
+            (((1,), (1,)), ((), ())),
+            preferred_element_type=jnp.float32,
+        )
         + bias_ref[...]
     )
-    out_ref[...] = velocity
+    conditional, unconditional = velocity[:half], velocity[half:]
+    out_ref[...] = unconditional + guide_ref[0] * (conditional - unconditional)
 
     for copy in pair_copies:
         copy.wait_send()
@@ -301,27 +319,25 @@
     half = rows // 2
     outs = head_weight.shape[1]
     tokens = chips * rows
-    branches, videos, text, share = text_keys.shape
-    slots = videos * text
+    _, videos, text, _ = text_keys.shape
     bf16, f32 = jnp.bfloat16, jnp.float32
     anywhere = pl.BlockSpec(memory_space=pl.ANY)
     scalar = pl.BlockSpec(memory_space=pltpu.SMEM)
     vector = pl.BlockSpec(memory_space=pltpu.VMEM)
-    velocity = pl.pallas_call(
+    return pl.pallas_call(
         functools.partial(kernel, n),
-        out_shape=jax.ShapeDtypeStruct((rows, outs), f32),
-        in_specs=[anywhere] * 6 + [scalar] * 2 + [vector] * 4,
+        out_shape=jax.ShapeDtypeStruct((half, outs), f32),
+        in_specs=[anywhere] * 6 + [scalar] * 2 + [vector] * 4 + [scalar],
         out_specs=vector,
         scratch_shapes=[
             pltpu.VMEM((tokens, HEAD_CHANNELS), bf16),
             pltpu.VMEM((tokens, HEAD_CHANNELS), bf16),
             pltpu.VMEM((tokens, HEAD_CHANNELS), bf16),
             pltpu.VMEM((tokens, HEAD_CHANNELS), bf16),
-            pltpu.VMEM((tokens, HEAD_CHANNELS), bf16),
-            pltpu.VMEM((2, slots, share), bf16),
-            pltpu.VMEM((2, slots, share), bf16),
-            pltpu.VMEM((slots, 2 * HEAD_CHANNELS), bf16),
-            pltpu.VMEM((slots, HEAD_CHANNELS), bf16),
+            pltpu.VMEM((2 * HEAD_CHANNELS, tokens), bf16),
+            pltpu.VMEM((videos, 2 * HEAD_CHANNELS, text), bf16),
+            pltpu.VMEM((videos, HEAD_CHANNELS, text), bf16),
+            pltpu.VMEM((videos * text, HEAD_CHANNELS), bf16),
             pltpu.VMEM((tokens, tokens), bf16),
             pltpu.VMEM((tokens, HEAD_CHANNELS), f32),
             pltpu.VMEM((tokens, HEAD_CHANNELS), bf16),
@@ -344,17 +360,16 @@
         self_keys,
         self_values,
         residual_in,
-        text_keys.reshape(branches, slots, share),
-        text_values.reshape(branches, slots, share),
+        text_keys.transpose(0, 1, 3, 2),
+        text_values.transpose(0, 1, 3, 2),
         text_lengths,
         frame_counts,
         mod_gain.reshape(1, features),
         mod_shift.reshape(1, features),
-        head_weight,
+        head_weight.T,
         head_bias.reshape(1, outs),
-    )
-    conditional, unconditional = velocity[:half], velocity[half:]
-    return unconditional + guide_scale[0] * (conditional - unconditional)
+        guide_scale,
+    )
 
 
 def solution(mesh):

time: 38.1 us -> 33.5 us (0.88)
  local copies, waits for them, and re-layouts: 3.85 us -> 1.35 us
  other arithmetic: 1.37 us -> 0 us
  Pallas kernels: 32 us -> 31.3 us
    unnamed x7 -> x1, local copies, waits for them, and re-layouts: 3.85 us -> 1.35 us
    add x1 -> x0, other arithmetic: 1.37 us -> none  [local(): return unconditional + guide_scale[0] * (conditional - unconditional)]
    pallas_call x1, Pallas kernels: 32 us -> 31.3 us  [local(): pl.pallas_call(functools.partial(kernel, n), out_shape=jax.ShapeDtypeStru...]
where the time goes in v2:
time: 33.5 us; the launch traced here: 33.3 us
  Pallas kernels  31.3 us (93%)
  local copies, waits for them, and re-layouts  1.35 us (4%)
  between operations  0.66 us (2%)
    pallas_call x1, Pallas kernels, local(): pl.pallas_call(functools.partial(kernel, n), out_shape=jax.ShapeDtypeStru...  31.3 us
    unnamed x1, local copies, waits for them, and re-layouts  1.35 us

profile of v2, /device:TPU:0, one launch (start us, length us, event | category | flops | bytes accessed | tf_op | source)
XLA Modules:
  0.0 33.3 jit_solution(15753542585379586521)
XLA Ops:
  0.7 31.3 %guided_block.1 = f32[48,64]{1,0:T(8,128)} custom-call(bf16[96,1024]{1,0:T(8,128)(2,1)} %q_ref.1, bf16[96,1024]{1,0:T(8,128)(2,1)} %k_ref.1, bf16[96,1024]{1,0:T(8,128)(2,1)} %v_ref.1, bf16[96,1024]{1,0:T(8,128)(2,1)} %x_ref.1, bf16[2,4,64,256]{3,2,1,0:T(8,128)(2,1)} %bitcast.6, bf16[2,4,64,256]{3,2,1,0:T(8,128)(2,1)} %bitcast.7, s32[2,4]{1,0:T(2,128)} %lengths_ref.1, ...), custom_call_target="tpu_custom_call" | custom-call | tf_op jit(solution)/shard_map/guided_block/pallas_call | solution.py:327
  32.0 1.3 %copy.16 = f32[48,64]{1,0:T(8,128)} copy(f32[48,64]{1,0:T(8,128)} %guided_block.1) | data formatting | bytes 24576

commit v3 on v2

--- a/solution.py
+++ b/solution.py
@@ -80,6 +80,11 @@
     tokens = chips * rows
     videos = frames_ref.shape[0]
     share, text = tk_ref.shape[2:]
+    paired = chips & (chips - 1) == 0
+
+    def far_first(step):
+        return chip ^ (chips - step) if paired else lax.rem(chip + step, chips)
+
     sources = (q_ref, k_ref, v_ref)
     landings = (qb, kb, vb)
 
@@ -155,7 +160,7 @@
 
         @pl.loop(1, chips)
         def _(step, which=which):
-            qkv_copy(which, lax.rem(chip + step, chips)).start()
+            qkv_copy(which, far_first(step)).start()
 
         if which < 2:
             pair_copies[which + 1].start()
@@ -186,28 +191,45 @@
     pair_wait(0)
     pair_wait(1)
     for f in range(videos):
-        t_vals[f * text : (f + 1) * text, :] = t_vals_in[f].T
+        t_vals[f] = t_vals_in[f].T
 
     def query_block(index):
         place = block(index, rows)
         return jnp.concatenate([qb[place, :], q_hot[place, :]], axis=-1)
 
+    def cross_of(index, queries):
+        frames = rows // TPF
+        picked = []
+        for i in range(frames):
+            frame = (index * frames + i) * TPF
+            video = jnp.int32(0)
+            for end in ends[:-1]:
+                video = video + jnp.where(frame >= end, 1, 0)
+            picked.append(video)
+        parts = [slice(i * TPF, (i + 1) * TPF) for i in range(frames)]
+        weights = weights_of(
+            jnp.concatenate(
+                [
+                    jnp.dot(queries[part], t_keys[video], preferred_element_type=jnp.float32)
+                    for part, video in zip(parts, picked)
+                ],
+                axis=0,
+            )
+        )
+        return jnp.concatenate(
+            [
+                jnp.dot(weights[part], t_vals[video], preferred_element_type=jnp.float32)
+                for part, video in zip(parts, picked)
+            ],
+            axis=0,
+        )
+
     @pl.loop(0, chips)
     def _(step):
         index = lax.rem(chip + step, chips)
         qkv_wait(0, index)
         queries = query_block(index)
-        scores = jnp.concatenate(
-            [
-                jnp.dot(queries, t_keys[f], preferred_element_type=jnp.float32)
-                for f in range(videos)
-            ],
-            axis=-1,
-        )
-        weights = weights_of(scores)
-        cross[block(index, rows), :] = jnp.dot(
-            weights, t_vals[...], preferred_element_type=jnp.float32
-        )
+        cross[block(index, rows), :] = cross_of(index, queries)
 
     @pl.loop(0, chips)
     def _(step):
@@ -215,7 +237,7 @@
 
     keys[:HEAD_CHANNELS, :] = kb[...].T
 
-    @pl.loop(0, chips)
+    @pl.loop(0, chips, unroll=4)
     def _(step):
         index = lax.rem(chip + step, chips)
         scores = jnp.dot(query_block(index), keys[...], preferred_element_type=jnp.float32)
@@ -242,7 +264,7 @@
             out_recv.at[me],
         )
 
-    @pl.loop(0, chips)
+    @pl.loop(0, chips, unroll=4)
     def _(step):
         index = lax.rem(chip + 1 + step, chips)
         place = block(index, rows)
@@ -326,7 +348,7 @@
     vector = pl.BlockSpec(memory_space=pltpu.VMEM)
     return pl.pallas_call(
         functools.partial(kernel, n),
-        out_shape=jax.ShapeDtypeStruct((half, outs), f32),
+        out_shape=pltpu.VMEM((half, outs), f32),
         in_specs=[anywhere] * 6 + [scalar] * 2 + [vector] * 4 + [scalar],
         out_specs=vector,
         scratch_shapes=[
@@ -337,7 +359,7 @@
             pltpu.VMEM((2 * HEAD_CHANNELS, tokens), bf16),
             pltpu.VMEM((videos, 2 * HEAD_CHANNELS, text), bf16),
             pltpu.VMEM((videos, HEAD_CHANNELS, text), bf16),
-            pltpu.VMEM((videos * text, HEAD_CHANNELS), bf16),
+            pltpu.VMEM((videos, text, HEAD_CHANNELS), bf16),
             pltpu.VMEM((tokens, tokens), bf16),
             pltpu.VMEM((tokens, HEAD_CHANNELS), f32),
             pltpu.VMEM((tokens, HEAD_CHANNELS), bf16),

time: 33.5 us -> 29.5 us (0.88)
  Pallas kernels: 31.3 us -> 28.1 us
  local copies, waits for them, and re-layouts: 1.35 us -> 0.61 us
    pallas_call x1, Pallas kernels: 31.3 us -> 28.1 us  [local(): pl.pallas_call(functools.partial(kernel, n), out_shape=pltpu.VMEM((half,...]
    unnamed x1, local copies, waits for them, and re-layouts: 1.35 us -> 0.61 us
where the time goes in v3:
time: 29.5 us; the launch traced here: 29.4 us
  Pallas kernels  28.1 us (95%)
  between operations  0.66 us (2%)
  local copies, waits for them, and re-layouts  0.61 us (2%)
    pallas_call x1, Pallas kernels, local(): pl.pallas_call(functools.partial(kernel, n), out_shape=pltpu.VMEM((half,...  28.1 us
    unnamed x1, local copies, waits for them, and re-layouts  0.61 us

profile of v3, /device:TPU:0, one launch (start us, length us, event | category | flops | bytes accessed | tf_op | source)
XLA Modules:
  0.0 29.4 jit_solution(15001302842463121113)
XLA Ops:
  0.7 28.1 %guided_block.1 = f32[48,64]{1,0:T(8,128)S(1)} custom-call(bf16[96,1024]{1,0:T(8,128)(2,1)} %q_ref.1, bf16[96,1024]{1,0:T(8,128)(2,1)} %k_ref.1, bf16[96,1024]{1,0:T(8,128)(2,1)} %v_ref.1, bf16[96,1024]{1,0:T(8,128)(2,1)} %x_ref.1, bf16[2,4,64,256]{3,2,1,0:T(8,128)(2,1)} %bitcast.6, bf16[2,4,64,256]{3,2,1,0:T(8,128)(2,1)} %bitcast.7, s32[2,4]{1,0:T(2,128)} %lengths_ref.1, ...), custom_call_target="tpu_custom_call" | custom-call | tf_op jit(solution)/shard_map/guided_block/pallas_call | solution.py:349
  28.8 0.6 %copy.15 = f32[48,64]{1,0:T(8,128)} copy(f32[48,64]{1,0:T(8,128)S(1)} %guided_block.1) | data formatting | bytes 24576

commit v4 on v3

--- a/solution.py
+++ b/solution.py
@@ -70,6 +70,7 @@
     out_send,
     out_recv,
     here_sem,
+    late_sem,
 ):
     me = lax.axis_index("seq")
     chips = n // 2
@@ -142,28 +143,67 @@
 
     barrier = pltpu.get_barrier_semaphore()
 
-    @pl.loop(1, n)
-    def _(step):
+    early = (chips - chips // 4) * 2
+    is_early = me < early
+
+    def greet(semaphore, device):
         pl.semaphore_signal(
-            barrier, inc=1, device_id={"seq": lax.rem(me + step, n)}, device_id_type=MESH_ID
-        )
+            semaphore, inc=1, device_id={"seq": device}, device_id_type=MESH_ID
+        )
+
+    @pl.when(is_early)
+    def _():
+        @pl.loop(1, n)
+        def _(step):
+            greet(barrier, lax.rem(me + step, n))
+
+    @pl.when(jnp.logical_not(is_early))
+    def _():
+        @pl.loop(early, n)
+        def _(device):
+            @pl.when(device != me)
+            def _():
+                greet(barrier, device)
 
     for copy in here_copies:
         copy.start()
     for which in range(3):
         own_copy(which).start()
 
-    pl.semaphore_wait(barrier, n - 1)
-
-    pair_copies[0].start()
-    for which in range(3):
-
+    def send_all(which):
         @pl.loop(1, chips)
-        def _(step, which=which):
+        def _(step):
             qkv_copy(which, far_first(step)).start()
 
-        if which < 2:
-            pair_copies[which + 1].start()
+    def send_group(which, to_early):
+        @pl.loop(1, chips)
+        def _(step):
+            peer = far_first(step)
+
+            @pl.when((peer * 2 < early) == to_early)
+            def _():
+                qkv_copy(which, peer).start()
+
+    @pl.when(is_early)
+    def _():
+        pl.semaphore_wait(barrier, early - 1)
+        pair_copies[0].start()
+        for which in range(1):
+            send_group(which, True)
+        pair_copies[1].start()
+
+    @pl.when(jnp.logical_not(is_early))
+    def _():
+        pl.semaphore_wait(barrier, n - 1)
+
+        @pl.loop(0, early)
+        def _(device):
+            greet(late_sem, device)
+
+        pair_copies[0].start()
+        for which in range(1):
+            send_all(which)
+        pair_copies[1].start()
 
     starts, ends, position = [], [], jnp.int32(0)
     for f in range(videos):
@@ -187,6 +227,16 @@
     def pair_wait(i):
         here_copies[i].wait()
         pair_copies[i].wait_recv()
+
+    @pl.when(is_early)
+    def _():
+        pl.semaphore_wait(late_sem, n - early)
+        for which in range(1):
+            send_group(which, False)
+
+    for which in range(1, 3):
+        send_all(which)
+    pair_copies[2].start()
 
     pair_wait(0)
     pair_wait(1)
@@ -372,6 +422,7 @@
             pltpu.SemaphoreType.DMA((n,)),
             pltpu.SemaphoreType.DMA((n,)),
             pltpu.SemaphoreType.DMA((3,)),
+            pltpu.SemaphoreType.REGULAR,
         ],
         compiler_params=pltpu.CompilerParams(
             collective_id=0, has_side_effects=True, vmem_limit_bytes=60 * 1024 * 1024

time: 29.5 us -> 28.7 us (0.973)
  Pallas kernels: 28.1 us -> 27.3 us
    pallas_call x1, Pallas kernels: 28.1 us -> 27.3 us  [local(): pl.pallas_call(functools.partial(kernel, n), out_shape=pltpu.VMEM((half,...]
where the time goes in v4:
time: 28.7 us; the launch traced here: 28.6 us
  Pallas kernels  27.3 us (95%)
  between operations  0.66 us (2%)
  local copies, waits for them, and re-layouts  0.61 us (2%)
    pallas_call x1, Pallas kernels, local(): pl.pallas_call(functools.partial(kernel, n), out_shape=pltpu.VMEM((half,...  27.3 us
    unnamed x1, local copies, waits for them, and re-layouts  0.61 us

profile of v4, /device:TPU:0, one launch (start us, length us, event | category | flops | bytes accessed | tf_op | source)
XLA Modules:
  0.0 28.6 jit_solution(12815644971588824162)
XLA Ops:
  0.7 27.3 %guided_block.1 = f32[48,64]{1,0:T(8,128)S(1)} custom-call(bf16[96,1024]{1,0:T(8,128)(2,1)} %q_ref.1, bf16[96,1024]{1,0:T(8,128)(2,1)} %k_ref.1, bf16[96,1024]{1,0:T(8,128)(2,1)} %v_ref.1, bf16[96,1024]{1,0:T(8,128)(2,1)} %x_ref.1, bf16[2,4,64,256]{3,2,1,0:T(8,128)(2,1)} %bitcast.6, bf16[2,4,64,256]{3,2,1,0:T(8,128)(2,1)} %bitcast.7, s32[2,4]{1,0:T(2,128)} %lengths_ref.1, ...), custom_call_target="tpu_custom_call" | custom-call | tf_op jit(solution)/shard_map/guided_block/pallas_call | solution.py:399
  27.9 0.6 %copy.15 = f32[48,64]{1,0:T(8,128)} copy(f32[48,64]{1,0:T(8,128)S(1)} %guided_block.1) | data formatting | bytes 24576

commit v5 on v4

--- a/solution.py
+++ b/solution.py
@@ -71,6 +71,7 @@
     out_recv,
     here_sem,
     late_sem,
+    weight_here,
 ):
     me = lax.axis_index("seq")
     chips = n // 2
@@ -124,6 +125,7 @@
         (tk_ref.at[core], key_place),
         (tv_ref.at[core], value_place),
         (x_ref.at[block(core, half)], xb.at[core]),
+        (weight_ref, weight_here),
     )
     pair_copies = [
         pltpu.make_async_remote_copy(
@@ -334,6 +336,7 @@
                 out_own().start()
 
     pair_wait(2)
+    here_copies[3].wait()
 
     @pl.loop(0, n)
     def _(device):
@@ -348,7 +351,7 @@
     velocity = (
         lax.dot_general(
             normed.astype(jnp.bfloat16),
-            weight_ref[...],
+            weight_here[...],
             (((1,), (1,)), ((), ())),
             preferred_element_type=jnp.float32,
         )
@@ -399,7 +402,7 @@
     return pl.pallas_call(
         functools.partial(kernel, n),
         out_shape=pltpu.VMEM((half, outs), f32),
-        in_specs=[anywhere] * 6 + [scalar] * 2 + [vector] * 4 + [scalar],
+        in_specs=[anywhere] * 6 + [scalar] * 2 + [vector] * 2 + [anywhere] + [vector] + [scalar],
         out_specs=vector,
         scratch_shapes=[
             pltpu.VMEM((tokens, HEAD_CHANNELS), bf16),
@@ -421,8 +424,9 @@
             pltpu.SemaphoreType.DMA((3,)),
             pltpu.SemaphoreType.DMA((n,)),
             pltpu.SemaphoreType.DMA((n,)),
-            pltpu.SemaphoreType.DMA((3,)),
+            pltpu.SemaphoreType.DMA((4,)),
             pltpu.SemaphoreType.REGULAR,
+            pltpu.VMEM((outs, features), bf16),
         ],
         compiler_params=pltpu.CompilerParams(
             collective_id=0, has_side_effects=True, vmem_limit_bytes=60 * 1024 * 1024

time: 28.7 us -> 28.5 us (level)
  no operation moved by 1% of the time
where the time goes in v5:
time: 28.5 us; the launch traced here: 28.4 us
  Pallas kernels  27.1 us (95%)
  between operations  0.66 us (2%)
  local copies, waits for them, and re-layouts  0.61 us (2%)
    pallas_call x1, Pallas kernels, local(): pl.pallas_call(functools.partial(kernel, n), out_shape=pltpu.VMEM((half,...  27.1 us
    unnamed x1, local copies, waits for them, and re-layouts  0.61 us

profile of v5, /device:TPU:0, one launch (start us, length us, event | category | flops | bytes accessed | tf_op | source)
XLA Modules:
  0.0 28.4 jit_solution(3852226902335349022)
XLA Ops:
  0.7 27.1 %guided_block.1 = f32[48,64]{1,0:T(8,128)S(1)} custom-call(bf16[96,1024]{1,0:T(8,128)(2,1)} %q_ref.1, bf16[96,1024]{1,0:T(8,128)(2,1)} %k_ref.1, bf16[96,1024]{1,0:T(8,128)(2,1)} %v_ref.1, bf16[96,1024]{1,0:T(8,128)(2,1)} %x_ref.1, bf16[2,4,64,256]{3,2,1,0:T(8,128)(2,1)} %bitcast.6, bf16[2,4,64,256]{3,2,1,0:T(8,128)(2,1)} %bitcast.7, s32[2,4]{1,0:T(2,128)} %lengths_ref.1, ...), custom_call_target="tpu_custom_call" | custom-call | tf_op jit(solution)/shard_map/guided_block/pallas_call | solution.py:402
  27.8 0.6 %copy.15 = f32[48,64]{1,0:T(8,128)} copy(f32[48,64]{1,0:T(8,128)S(1)} %guided_block.1) | data formatting | bytes 24576
